TPU v7x, 32 devices: a whole 2x2x4 slice. The times are simulated.
32 devices in a mesh: row: 8 (over y, x, core), col: 4 (over z).
Axes of the slice: x: 2, y: 2, z: 4, core: 2. Of those that a mesh axis runs over, the one named last changes fastest.
Arguments:
- hidden_in: bfloat16 [1152, 2048], P('col', 'row'), may hold values from -21 to 21
- state: float32 [128, 2048, 1152], P('col', 'row'), may hold values from -4 to 4
- attn_norm_gain: bfloat16 [2048], replicated, may hold values from 0.099609375 to 1.8984375
- w_query: bfloat16 [2048, 2048], P(None, 'row'), may hold values from -0.125 to 0.125
- w_key: bfloat16 [2048, 2048], P(None, 'row'), may hold values from -0.125 to 0.125
- w_value: bfloat16 [2048, 2048], P(None, 'row'), may hold values from -0.125 to 0.125
- w_gate: bfloat16 [2048, 2048], P(None, 'row'), may hold values from -0.125 to 0.125
- w_decay: bfloat16 [2048, 16], replicated, may hold values from -0.125 to 0.125
- w_beta: bfloat16 [2048, 16], replicated, may hold values from -0.125 to 0.125
- decay_log: float32 [16], replicated, may hold values from -3 to 1.5
- decay_bias: float32 [16], replicated, may hold values from -2 to 1
- head_gain: float32 [128], replicated, may hold values from 0.1 to 1.9
- w_out: bfloat16 [2048, 2048], P('row'), may hold values from -0.125 to 0.125
- final_gain: bfloat16 [2048], P('row'), may hold values from 0.099609375 to 1.8984375
- lm_weight: bfloat16 [2048, 20480], P(None, ('row', 'col')), may hold values from -0.28726213 to 0.28726213
- token_ids: int32 [1152], replicated, may hold values from 0 to 20479
- ref_logprob: float32 [1152], replicated, may hold values from -16 to -6
Outputs:
- new_state: float32 [128, 2048, 1152], P('col', 'row')
- logprob: float32 [1152], replicated
- entropy: float32 [1152], replicated
- kl: float32 [1152], replicated
All inputs are finite; a program needn't handle non-finite values.
Results may differ from a plain program's by a relative error of at most 0.0014.
The roundings to bfloat16 on the way count: a program that leaves them out, or rounds other values in their place, can miss the bound.
Values may be sent and summed in bfloat16 or wider, within the bound.
A program may use at most 128 MiB of HBM per device.

v0:
```python
import jax
import jax.numpy as jnp
from jax import lax
from jax.sharding import PartitionSpec as P

D = 2048
HEADS = 16
DK = 128
DV = 128


def partner_2(block, axis, apart):
    count = lax.axis_size(axis)
    route = []
    for low in range(count):
        high = low | 1 << apart
        if high != low and high < count:
            route += [(low, high), (high, low)]
    return lax.ppermute(block, axis, route)


def project(weight, normed):
    return lax.dot_general(
        weight, normed, (((0,), (1,)), ((), ())), preferred_element_type=jnp.float32
    )


def per_device(
    hidden_in,
    state,
    attn_norm_gain,
    w_query,
    w_key,
    w_value,
    w_gate,
    w_decay,
    w_beta,
    decay_log,
    decay_bias,
    head_gain,
    w_out,
    final_gain,
    lm_weight,
    token_ids,
    ref_logprob,
):
    highest = lax.Precision.HIGHEST
    row_count = lax.axis_size("row")
    col_count = lax.axis_size("col")
    row_index = lax.axis_index("row")
    col_index = lax.axis_index("col")
    group = max(1, row_count // HEADS)
    local_heads = max(1, HEADS // row_count)
    first_head = row_index // group * local_heads
    value_cols = w_value.shape[1]
    value_part = value_cols // local_heads
    block_rows = hidden_in.shape[0]
    key_rows = state.shape[0]
    batch = state.shape[2]
    vocab_dev = lm_weight.shape[1]
    whole_rows = lax.all_gather(hidden_in, "row", axis=1, tiled=True)
    xfull = whole_rows.astype(jnp.float32)
    normed = (
        xfull
        * lax.rsqrt(jnp.mean(xfull * xfull, axis=1, keepdims=True) + 1e-06)
        * attn_norm_gain.astype(jnp.float32)
    ).astype(jnp.bfloat16)
    raw_pair = jnp.stack([project(w_query, normed), project(w_key, normed)]).astype(jnp.bfloat16)
    raw_pair = lax.optimization_barrier(raw_pair)
    for level in range(group.bit_length() - 1):
        partner = partner_2(raw_pair, "row", level)
        upper = row_index >> level & 1 == 1
        raw_pair = jnp.where(
            upper,
            jnp.concatenate([partner, raw_pair], axis=1),
            jnp.concatenate([raw_pair, partner], axis=1),
        )
    pair_f = raw_pair.astype(jnp.float32).reshape(2, local_heads, DK, block_rows)
    unit_pair = (
        pair_f * lax.rsqrt(jnp.sum(pair_f * pair_f, axis=2, keepdims=True) + 1e-06)
    ).astype(jnp.bfloat16)
    tiles_qk = lax.all_to_all(unit_pair, "col", split_axis=2, concat_axis=3, tiled=True)
    query = tiles_qk[0].astype(jnp.float32)
    key = tiles_qk[1].astype(jnp.float32)
    value_t = project(w_value, normed)
    gate_t = project(w_gate, normed)
    decay_in = lax.dynamic_slice_in_dim(project(w_decay, normed), first_head, local_heads, 0)
    beta_in = lax.dynamic_slice_in_dim(project(w_beta, normed), first_head, local_heads, 0)
    rate = jnp.exp(lax.dynamic_slice_in_dim(decay_log, first_head, local_heads, 0))
    bias = lax.dynamic_slice_in_dim(decay_bias, first_head, local_heads, 0)
    alpha_t = jnp.exp(-rate[:, None] * jax.nn.softplus(decay_in + bias[:, None]))
    beta_t = jax.nn.sigmoid(beta_in)
    value_all, gate_all, alpha, beta = (
        lax.all_gather(value_t, "col", axis=1, tiled=True),
        lax.all_gather(gate_t, "col", axis=1, tiled=True),
        lax.all_gather(alpha_t, "col", axis=1, tiled=True),
        lax.all_gather(beta_t, "col", axis=1, tiled=True),
    )
    tiles = state.reshape(key_rows, local_heads, value_part, batch)
    value4 = value_all.reshape(local_heads, value_part, batch)
    key_major = jnp.transpose(key, (1, 0, 2))
    recall, answer, intersection = lax.psum(
        (
            jnp.einsum("khvb,hkb->hvb", tiles, key, precision=highest),
            jnp.einsum("khvb,hkb->hvb", tiles, query, precision=highest),
            jnp.sum(key * query, axis=1),
        ),
        "col",
    )
    write = beta[:, None, :] * (value4 - alpha[:, None, :] * recall)
    updated = alpha[None, :, None, :] * tiles + key_major[:, :, None, :] * write[None]
    readout = alpha[:, None, :] * answer + intersection[:, None, :] * write
    power = jnp.sum(readout * readout, axis=1)
    for level in range(group.bit_length() - 1):
        power = power + partner_2(power, "row", level)
    gain_part = lax.dynamic_slice_in_dim(head_gain, row_index % group * value_part, value_part, 0)
    gate4 = gate_all.reshape(local_heads, value_part, batch)
    mixed = (
        readout
        * lax.rsqrt(power / DV + 1e-05)[:, None, :]
        * gain_part[None, :, None]
        * jax.nn.silu(gate4)
    )
    mixed_heads = mixed.reshape(value_cols, batch).astype(jnp.bfloat16)
    mine = lax.dynamic_slice_in_dim(mixed_heads, col_index * block_rows, block_rows, 1)
    branch = lax.psum_scatter(
        lax.dot_general(w_out, mine, (((0,), (0,)), ((), ())), preferred_element_type=jnp.float32),
        "row",
        scatter_dimension=0,
        tiled=True,
    )
    hidden = hidden_in.astype(jnp.float32) + branch.T
    energy = lax.psum(jnp.sum(hidden * hidden, axis=1), "row")
    final = (
        hidden * lax.rsqrt(energy / D + 1e-06)[:, None] * final_gain.astype(jnp.float32)[None, :]
    ).astype(jnp.bfloat16)
    tall = lax.all_gather(final, "col", axis=0, tiled=True)
    logits = jnp.dot(
        lax.all_gather(tall, "row", axis=1, tiled=True),
        lm_weight,
        preferred_element_type=jnp.float32,
    )
    vocab_start = (row_index * col_count + col_index) * vocab_dev
    hits = jnp.arange(vocab_dev, dtype=jnp.int32)[None, :] + vocab_start == token_ids[:, None]
    local_pick = jnp.sum(jnp.where(hits, logits, jnp.zeros_like(logits)), axis=1)
    local_top = jnp.max(logits, axis=1)
    expo = jnp.exp(logits - local_top[:, None])
    local_total = jnp.sum(expo, axis=1)
    local_weighted = jnp.sum(expo * logits, axis=1)
    top = lax.pmax(local_top, ("row", "col"))
    shrink = jnp.exp(local_top - top)
    total, weighted, picked = lax.psum(
        (local_total * shrink, local_weighted * shrink, local_pick), ("row", "col")
    )
    lse = top + jnp.log(total)
    logprob = picked - lse
    entropy = lse - weighted / total
    gap = jnp.clip(ref_logprob - logprob, -20.0, 20.0)
    kl = jnp.minimum(jnp.exp(gap) - gap - 1.0, 10.0)
    new_state = updated.reshape(key_rows, value_cols, batch)
    return (new_state, logprob, entropy, kl)


def solution(mesh):
    in_specs = (
        P("col", "row"),
        P("col", "row", None),
        P(),
        P(None, "row"),
        P(None, "row"),
        P(None, "row"),
        P(None, "row"),
        P(),
        P(),
        P(),
        P(),
        P(),
        P("row", None),
        P("row"),
        P(None, ("row", "col")),
        P(),
        P(),
    )
    out_specs = (P("col", "row", None), P(), P(), P())
    return jax.shard_map(
        per_device, mesh=mesh, in_specs=in_specs, out_specs=out_specs, check_vma=False
    )
```

profile of v0, /device:TPU:0, one launch (start us, length us, event | category | flops | bytes accessed | tf_op | source)
XLA Modules:
  0.0 437.5 jit_solution(9611972325087262936)
XLA Ops:
  8.7 28.0 %all-gather.7.cloned.1.call-done = bf16[288,2048]{1,0:T(8,128)(2,1)} async-done(((bf16[288,256]{1,0:T(8,128)(2,1)}), bf16[288,2048]{1,0:T(8,128)(2,1)}) %all-gather.7.cloned.1.call-update) | async-done | bytes 1179664 | tf_op jit(solution)/shard_map/all_gather | solution.py:61
  47.9 4.6 %all-to-all-start = ((bf16[2,2,128,288]{3,1,0,2:T(2,128)(2,1)}), bf16[2,2,128,288]{3,1,0,2:T(2,128)(2,1)S(1)}, u32[]{:S(2)}, u32[]{:S(2)}) async-start(bf16[2,2,128,288]{3,1,0,2:T(2,128)(2,1)} %copy.81), calls=%async_computation | async-start | bytes 786432 | tf_op jit(solution)/shard_map/all_to_all | solution.py:82
  52.5 2.8 convolution_bitcast_fusion.1
  55.4 20.5 %all-to-all-done = bf16[2,2,128,288]{3,1,0,2:T(2,128)(2,1)S(1)} async-done(((bf16[2,2,128,288]{3,1,0,2:T(2,128)(2,1)}), bf16[2,2,128,288]{3,1,0,2:T(2,128)(2,1)S(1)}, u32[]{:S(2)}, u32[]{:S(2)}) %all-to-all-start) | async-done | bytes 294944 | tf_op jit(solution)/shard_map/all_to_all | solution.py:82
  77.9 17.6 %multiply_reduce_fusion = (f32[2,1152,128]{1,2,0:T(8,128)}, f32[2,1152,128]{1,2,0:T(8,128)}) fusion(f32[2,1152,32,128]{1,3,0,2:T(8,128)} %bitcast.104, f32[2,1152,32]{1,0,2:T(2,128)S(1)} %copy.112, f32[2,1152,32]{1,0,2:T(2,128)S(1)} %copy.111), kind=kLoop, calls=%fused_computation.2 | loop fusion | flops 37158912 | bytes 40697856
  95.5 3.3 copy.107
  98.8 3.4 copy.99
  104.8 13.3 %all-gather.1 = f32[4,288,2]{1,2,0:T(2,128)S(1)} all-gather(f32[1,288,2]{1,2,0:T(2,128)S(1)} %divide_bitcast_fusion), channel_id=1, replica_groups=mesh['row'=8,'col'=4] {'col'}, dimensions={0}, use_global_device_ids=true | all-gather | bytes 11520 | tf_op jit(solution)/shard_map/all_gather | solution.py:97
  120.1 13.7 %all-gather = f32[4,288,2]{1,2,0:T(2,128)S(1)} all-gather(f32[1,288,2]{1,2,0:T(2,128)S(1)} %fusion.18), channel_id=1, replica_groups=mesh['row'=8,'col'=4] {'col'}, dimensions={0}, use_global_device_ids=true | all-gather | bytes 11520 | tf_op jit(solution)/shard_map/all_gather | solution.py:96
  136.4 11.1 %psum.51 = f32[2,1152]{1,0:T(2,128)S(1)} all-reduce(f32[2,1152]{1,0:T(2,128)S(1)} %reduce_sum.77), channel_id=1, replica_groups=mesh['row'=8,'col'=4] {'col'}, use_global_device_ids=true, to_apply=%region_5.6 | all-reduce | flops 2304 | bytes 18432 | tf_op jit(solution)/shard_map/psum | solution.py:102
  148.6 2.8 reshape.76
  151.4 2.8 reshape.78
  154.2 54.1 %all-reduce.4.cloned.1.call-done = (f32[2,128,1152]{1,0,2:T(2,128)}, f32[2,128,1152]{1,0,2:T(2,128)}) async-done(((f32[2,128,1152]{1,0,2:T(2,128)}, f32[2,128,1152]{1,0,2:T(2,128)}), (f32[2,128,1152]{1,0,2:T(2,128)}, f32[2,128,1152]{1,0,2:T(2,128)})) %all-reduce.4.cloned.1.call-update) | async-done | bytes 2359312 | tf_op jit(solution)/shard_map/psum | solution.py:102
  208.2 7.9 %multiply_reduce_fusion.3 = (f32[2,1152]{0,1:T(8,128)S(1)}, f32[2,128,1152]{1,0,2:T(2,128)S(1)}) fusion(f32[2,1152]{0,1:T(8,128)} %copy.89, f32[2,128,1152]{1,0,2:T(2,128)} %get-tuple-element.13, f32[2,1152]{0,1:T(8,128)S(1)} %copy.77, f32[2,128,1152]{1,0,2:T(2,128)} %reshape.76, f32[2,128,1152]{1,0,2:T(2,128)} %get-tuple-element.12, f32[2,1152]{0,1:T(8,128)} %copy.86), kind=kLoop, calls=%fused_computation.16 | loop fusion | flops 2356992 | bytes 4755456 | tf_op jit(solution)/shard_map/reduce_sum | solution.py:113
  217.6 4.6 %fusion.6 = bf16[2,128,1152]{1,0,2:T(2,128)(2,1)S(1)} fusion(f32[2,128,1152]{1,0,2:T(2,128)S(1)} %copy-done.7, f32[128]{0:T(128)S(1)} %copy-done.16, f32[2,1152]{0,1:T(8,128)S(1)} %add_rsqrt_fusion, f32[2,128,1152]{1,0,2:T(2,128)S(1)} %get-tuple-element.17, f32[2,1152]{0,1:T(8,128)S(1)} %copy-done.4, f32[2,128,1152]{1,0,2:T(2,128)S(1)} %copy-done.5, ...), kind=kLoop, calls=%fused_computation.19 | loop fusion | flops 3244032 | bytes 4156928 | tf_op jit(solution)/shard_map/convert_element_type | solution.py:124
  226.0 40.9 %reduce-scatter.2.cloned.1.call-done = f32[256,288]{0,1:T(8,128)} async-done(((f32[2048,288]{0,1:T(8,128)}), f32[256,288]{0,1:T(8,128)}) %reduce-scatter.2.cloned.1.call-update) | async-done | bytes 294928 | tf_op jit(solution)/shard_map/reduce_scatter | solution.py:126
  268.0 12.5 %psum.52 = f32[288]{0:T(512)S(1)} all-reduce(f32[288]{0:T(512)S(1)} %multiply_reduce_fusion.6), channel_id=1, replica_groups=mesh['row'=8,'col'=4] {'row'}, use_global_device_ids=true, to_apply=%region_9.10 | all-reduce | flops 288 | bytes 2304 | tf_op jit(solution)/shard_map/psum | solution.py:133
  281.6 16.7 %all_gather.26 = bf16[1152,256]{1,0:T(8,128)(2,1)} all-gather(bf16[288,256]{1,0:T(8,128)(2,1)S(1)} %multiply_convert_fusion), channel_id=1, replica_groups=mesh['row'=8,'col'=4] {'col'}, dimensions={0}, use_global_device_ids=true | all-gather | bytes 737280 | tf_op jit(solution)/shard_map/all_gather | solution.py:137
  298.6 3.4 copy.109
  303.2 28.9 %fusion = f32[32,256,1152]{2,1,0:T(8,128)} fusion(f32[32,256,1152]{2,1,0:T(8,128)} %param.18, f32[256,1152]{1,0:T(8,128)S(1)} %bitcast.107, f32[32,2,1152]{2,1,0:T(2,128)S(1)} %copy.84, f32[256,1152]{1,0:T(8,128)S(1)} %bitcast.108), kind=kLoop, calls=%fused_computation.1 | loop fusion | flops 28311552 | bytes 78151680 | tf_op jit(solution)/shard_map/add | solution.py:111
  332.1 6.9 %all-gather.13.cloned.1.call-done = bf16[1152,2048]{1,0:T(8,128)(2,1)} async-done(((bf16[1152,256]{1,0:T(8,128)(2,1)}), bf16[1152,2048]{1,0:T(8,128)(2,1)}) %all-gather.13.cloned.1.call-update) | async-done | bytes 4718608 | tf_op jit(solution)/shard_map/all_gather | solution.py:139
  339.0 7.6 %fusion.26 = (f32[1152]{0:T(1024)S(1)}, f32[1152,640]{0,1:T(8,128)}) fusion(bf16[1152,2048]{1,0:T(8,128)(2,1)} %all-gather.13.cloned.1.call-done, bf16[2048,640]{1,0:T(8,128)(2,1)S(1)} %copy-done), kind=kOutput, calls=%fused_computation.68 | convolution fusion | flops 3020635136 | bytes 10293760 | tf_op jit(solution)/shard_map/dot_general | solution.py:138
  346.6 39.3 %pmax.7 = f32[1152]{0:T(1024)S(1)} all-reduce(f32[1152]{0:T(1024)S(1)} %get-tuple-element.25), channel_id=1, replica_groups=mesh['row'=8,'col'=4] {'row','col'}, use_global_device_ids=true, to_apply=%region_13.14 | all-reduce | flops 1152 | bytes 9216 | tf_op jit(solution)/shard_map/pmax | solution.py:150
  388.7 41.3 %all-reduce = (f32[1152]{0:T(1024)S(1)}, f32[1152]{0:T(1024)S(1)}, f32[1152]{0:T(1024)S(1)}) all-reduce(f32[1152]{0:T(1024)S(1)} %get-tuple-element.8, f32[1152]{0:T(1024)S(1)} %get-tuple-element.24, f32[1152]{0:T(1024)S(1)} %get-tuple-element.23), channel_id=1, replica_groups=mesh['row'=8,'col'=4] {'row','col'}, use_global_device_ids=true, to_apply=%region_11.12 | all-reduce | flops 3456 | bytes 27648 | tf_op jit(solution)/shard_map/psum | solution.py:152
  (110 shorter events, 35.1 us)
Async XLA Ops:
  7.2 331.9 %copy-start = (bf16[2048,640]{1,0:T(8,128)(2,1)S(1)}, bf16[2048,640]{1,0:T(8,128)(2,1)}, u32[]{:S(2)}) copy-start(bf16[2048,640]{1,0:T(8,128)(2,1)} %param.31) | copy-start | bytes 7864324
  7.2 29.5 %all-gather.7.cloned.1.call-start = ((), (), s32[]{:S(2)}) async-start(), calls=%async_computation.2 | async-start | bytes 1327104 | tf_op jit(solution)/shard_map/all_gather | solution.py:61
  7.9 140.7 %all-gather.9.cloned.1.call-start = ((), (), s32[]{:S(2)}) async-start(), calls=%async_computation.3 | async-start | bytes 1474560 | tf_op jit(solution)/shard_map/all_gather | solution.py:94
  36.7 1.7 copy-start.6
  38.4 1.4 copy-start.17
  38.7 1.0 copy-start.2
  41.0 2.2 copy-start.3
  41.0 2.2 copy-start.18
  47.9 28.0 %all-to-all-start = ((bf16[2,2,128,288]{3,1,0,2:T(2,128)(2,1)}), bf16[2,2,128,288]{3,1,0,2:T(2,128)(2,1)S(1)}, u32[]{:S(2)}, u32[]{:S(2)}) async-start(bf16[2,2,128,288]{3,1,0,2:T(2,128)(2,1)} %copy.81), calls=%async_computation | async-start | bytes 786432 | tf_op jit(solution)/shard_map/all_to_all | solution.py:82
  52.5 98.8 %all-gather.11.cloned.1.call-start = ((), (), s32[]{:S(2)}) async-start(), calls=%async_computation.4 | async-start | bytes 1474560 | tf_op jit(solution)/shard_map/all_gather | solution.py:95
  55.4 152.9 %all-reduce.4.cloned.1.call-start = ((), (), s32[]{:S(2)}) async-start(), calls=%async_computation.7 | async-start | bytes 4718592 | tf_op jit(solution)/shard_map/psum | solution.py:102
  102.2 16.0 %copy-start.13 = (bf16[2048,16]{0,1:T(8,128)(2,1)S(1)}, bf16[2048,16]{0,1:T(8,128)(2,1)}, u32[]{:S(2)}) copy-start(bf16[2048,16]{0,1:T(8,128)(2,1)} %param.24) | copy-start | bytes 196612
  102.2 164.6 %reduce-scatter.2.cloned.1.call-start = ((), (), s32[]{:S(2)}) async-start(), calls=%async_computation.5 | async-start | bytes 2654208 | tf_op jit(solution)/shard_map/reduce_scatter | solution.py:126
  208.2 8.0 %copy-start.5 = (f32[2,128,1152]{1,0,2:T(2,128)S(1)}, f32[2,128,1152]{1,0,2:T(2,128)}, u32[]{:S(2)}) copy-start(f32[2,128,1152]{1,0,2:T(2,128)} %get-tuple-element.13) | copy-start | bytes 3538948
  208.2 8.0 %copy-start.7 = (f32[2,128,1152]{1,0,2:T(2,128)S(1)}, f32[2,128,1152]{1,0,2:T(2,128)}, u32[]{:S(2)}) copy-start(f32[2,128,1152]{1,0,2:T(2,128)} %reshape.78) | copy-start | bytes 3538948
  216.1 6.1 %copy-start.1 = (f32[2,128,1152]{1,0,2:T(2,128)}, f32[2,128,1152]{1,0,2:T(2,128)S(1)}, u32[]{:S(2)}) copy-start(f32[2,128,1152]{1,0,2:T(2,128)S(1)} %get-tuple-element.17) | copy-start | bytes 3538948
  216.1 1.5 copy-start.4
  216.1 1.5 copy-start.16
  222.2 1.2 copy-start.11
  225.3 41.5 %copy-start.10 = (bf16[288,256]{1,0:T(8,128)(2,1)S(1)}, bf16[288,256]{1,0:T(8,128)(2,1)}, u32[]{:S(2)}) copy-start(bf16[288,256]{1,0:T(8,128)(2,1)} %param.17) | copy-start | bytes 442372
  225.4 113.7 %all-gather.13.cloned.1.call-start = ((), (), s32[]{:S(2)}) async-start(), calls=%async_computation.6 | async-start | bytes 5308416 | tf_op jit(solution)/shard_map/all_gather | solution.py:139
  301.9 1.3 copy-start.8
  332.1 53.8 %copy-start.14 = (s32[1152]{0:T(1024)S(1)}, s32[1152]{0:T(1024)}, u32[]{:S(2)}) copy-start(s32[1152]{0:T(1024)} %param.32) | copy-start | bytes 13828
  385.9 44.1 %copy-start.15 = (f32[1152]{0:T(1024)S(1)}, f32[1152]{0:T(1024)}, u32[]{:S(2)}) copy-start(f32[1152]{0:T(1024)} %param.33) | copy-start | bytes 13828
  (5 other events, 3.7 us)
Sparse Core Ops, SparseCore 0:
  9.9 26.7 all-gather.6
  41.1 38.9 all-gather.8
  81.7 29.1 all-gather.10
  113.2 94.9 all-reduce.3
  225.5 41.3 reduce-scatter.1
  298.4 40.5 all-gather.12
where the time goes:
time: 439 us; the launch traced here: 437 us
  waiting for transfers between devices  151 us (34%)
  blocking collectives  148 us (34%)
  other arithmetic  70.4 us (16%)
  local copies, waits for them, and re-layouts  29.1 us (7%)
  matrix products  19.6 us (4%)
  between operations  14.5 us (3%)
  starting transfers between devices  4.8 us (1%)
    psum x1, waiting for transfers between devices, per_device(): lax.psum((jnp.einsum('khvb,hkb->hvb', tiles, key, precision=highest), jnp...  54.1 us
    psum x1, blocking collectives, per_device(): lax.psum((local_total * shrink, local_weighted * shrink, local_pick), ('r...  41.3 us
    reduce_scatter x1, waiting for transfers between devices, per_device(): lax.psum_scatter(lax.dot_general(w_out, mine, (((0,), (0,)), ((), ())), p...  40.9 us
    pmax x1, blocking collectives, per_device(): top = lax.pmax(local_top, ('row', 'col'))  39.3 us
    add x1, other arithmetic, per_device(): alpha[None, :, None, :] * tiles + key_major[:, :, None, :] * write[None]  28.9 us
    all_gather x1, waiting for transfers between devices, per_device(): whole_rows = lax.all_gather(hidden_in, 'row', axis=1, tiled=True)  28 us
    all_to_all x1, waiting for transfers between devices, per_device(): lax.all_to_all(unit_pair, 'col', split_axis=2, concat_axis=3, tiled=True)  20.5 us
    unnamed x4, other arithmetic  17.7 us
  transfers between devices with their start and end apart: 7, of which 5 were waited for; matrix products, arithmetic and copies ran while one was open for 19% of the time, Pallas kernels for 0%

commit v1 on v0

--- a/solution.py
+++ b/solution.py
@@ -58,7 +58,12 @@
     key_rows = state.shape[0]
     batch = state.shape[2]
     vocab_dev = lm_weight.shape[1]
-    whole_rows = lax.all_gather(hidden_in, "row", axis=1, tiled=True)
+    ring = [hidden_in]
+    for hop in range(7):
+        ring.append(lax.ppermute(ring[-1], "row", [(dev, (dev + 1) % 8) for dev in range(8)]))
+    whole_rows = jnp.roll(
+        jnp.concatenate(ring[::-1], axis=1), (lax.axis_index("row") + 1) * ring[0].shape[1], axis=1
+    )
     xfull = whole_rows.astype(jnp.float32)
     normed = (
         xfull

time: 439 us -> 449 us (1.023)
  waiting for transfers between devices: 151 us -> 161 us
    ppermute x0 -> x7, waiting for transfers between devices: none -> 38.4 us  [per_device(): lax.ppermute(ring[-1], 'row', [(dev, (dev + 1) % 8) for dev in range(8)])]
    all_gather x1 -> x0, waiting for transfers between devices: 28 us -> none  [per_device(): whole_rows = lax.all_gather(hidden_in, 'row', axis=1, tiled=True)]
    unnamed x51 -> x64, local copies, waits for them, and re-layouts: 8.76 us -> 9.04 us
  transfers between devices with their start and end apart: 7 -> 13, of which waited for: 5 -> 11; matrix products, arithmetic and copies ran while one was open for 19% -> 18% of each run, Pallas kernels for 0% -> 0%
where the time goes in v1:
time: 449 us; the launch traced here: 448 us
  waiting for transfers between devices  161 us (36%)
  blocking collectives  149 us (33%)
  other arithmetic  69.1 us (15%)
  local copies, waits for them, and re-layouts  29.4 us (7%)
  matrix products  19.5 us (4%)
  between operations  14.3 us (3%)
  starting transfers between devices  6.53 us (1%)
    psum x1, waiting for transfers between devices, per_device(): lax.psum((jnp.einsum('khvb,hkb->hvb', tiles, key, precision=highest), jnp...  55.5 us
    psum x1, blocking collectives, per_device(): lax.psum((local_total * shrink, local_weighted * shrink, local_pick), ('r...  41.3 us
    reduce_scatter x1, waiting for transfers between devices, per_device(): lax.psum_scatter(lax.dot_general(w_out, mine, (((0,), (0,)), ((), ())), p...  40.9 us
    pmax x1, blocking collectives, per_device(): top = lax.pmax(local_top, ('row', 'col'))  39.3 us
    ppermute x7, waiting for transfers between devices, per_device(): lax.ppermute(ring[-1], 'row', [(dev, (dev + 1) % 8) for dev in range(8)])  38.4 us
    add x1, other arithmetic, per_device(): alpha[None, :, None, :] * tiles + key_major[:, :, None, :] * write[None]  29 us
    unnamed x4, other arithmetic  17.7 us
    all_to_all x1, waiting for transfers between devices, per_device(): lax.all_to_all(unit_pair, 'col', split_axis=2, concat_axis=3, tiled=True)  17.7 us
  transfers between devices with their start and end apart: 13, of which 11 were waited for; matrix products, arithmetic and copies ran while one was open for 18% of the time, Pallas kernels for 0%

profile of v1, /device:TPU:0, one launch (start us, length us, event | category | flops | bytes accessed | tf_op | source)
XLA Modules:
  0.0 448.1 jit_solution(13755271509752090441)
XLA Ops:
  7.8 5.9 %collective-permute-done = bf16[288,256]{1,0:T(8,128)(2,1)S(1)} collective-permute-done((bf16[288,256]{1,0:T(8,128)(2,1)}, bf16[288,256]{1,0:T(8,128)(2,1)S(1)}, u32[]{:S(2)}, u32[]{:S(2)}) %collective-permute-start) | collective-permute-done | bytes 147488 | tf_op jit(solution)/shard_map/ppermute | solution.py:63
  13.7 5.5 %collective-permute-done.1 = bf16[288,256]{1,0:T(8,128)(2,1)S(1)} collective-permute-done((bf16[288,256]{1,0:T(8,128)(2,1)S(1)}, bf16[288,256]{1,0:T(8,128)(2,1)S(1)}, u32[]{:S(2)}, u32[]{:S(2)}) %collective-permute-start.1) | collective-permute-done | bytes 147488 | tf_op jit(solution)/shard_map/ppermute | solution.py:63
  19.2 5.5 %collective-permute-done.2 = bf16[288,256]{1,0:T(8,128)(2,1)S(1)} collective-permute-done((bf16[288,256]{1,0:T(8,128)(2,1)S(1)}, bf16[288,256]{1,0:T(8,128)(2,1)S(1)}, u32[]{:S(2)}, u32[]{:S(2)}) %collective-permute-start.2) | collective-permute-done | bytes 147488 | tf_op jit(solution)/shard_map/ppermute | solution.py:63
  24.6 5.5 %collective-permute-done.3 = bf16[288,256]{1,0:T(8,128)(2,1)S(1)} collective-permute-done((bf16[288,256]{1,0:T(8,128)(2,1)S(1)}, bf16[288,256]{1,0:T(8,128)(2,1)S(1)}, u32[]{:S(2)}, u32[]{:S(2)}) %collective-permute-start.3) | collective-permute-done | bytes 147488 | tf_op jit(solution)/shard_map/ppermute | solution.py:63
  30.1 5.5 %collective-permute-done.4 = bf16[288,256]{1,0:T(8,128)(2,1)S(1)} collective-permute-done((bf16[288,256]{1,0:T(8,128)(2,1)S(1)}, bf16[288,256]{1,0:T(8,128)(2,1)S(1)}, u32[]{:S(2)}, u32[]{:S(2)}) %collective-permute-start.4) | collective-permute-done | bytes 147488 | tf_op jit(solution)/shard_map/ppermute | solution.py:63
  35.6 5.6 %collective-permute-done.5 = bf16[288,256]{1,0:T(8,128)(2,1)} collective-permute-done((bf16[288,256]{1,0:T(8,128)(2,1)S(1)}, bf16[288,256]{1,0:T(8,128)(2,1)}, u32[]{:S(2)}, u32[]{:S(2)}) %collective-permute-start.5) | collective-permute-done | bytes 147488 | tf_op jit(solution)/shard_map/ppermute | solution.py:63
  41.8 5.1 %collective-permute-done.6 = bf16[288,256]{1,0:T(8,128)(2,1)} collective-permute-done((bf16[288,256]{1,0:T(8,128)(2,1)}, bf16[288,256]{1,0:T(8,128)(2,1)}, u32[]{:S(2)}, u32[]{:S(2)}) %collective-permute-start.6) | collective-permute-done | bytes 147488 | tf_op jit(solution)/shard_map/ppermute | solution.py:63
  61.7 5.6 %all-to-all-start = ((bf16[2,2,128,288]{3,1,0,2:T(2,128)(2,1)}), bf16[2,2,128,288]{3,1,0,2:T(2,128)(2,1)S(1)}, u32[]{:S(2)}, u32[]{:S(2)}) async-start(bf16[2,2,128,288]{3,1,0,2:T(2,128)(2,1)} %copy.81), calls=%async_computation | async-start | bytes 786432 | tf_op jit(solution)/shard_map/all_to_all | solution.py:87
  70.1 17.7 %all-to-all-done = bf16[2,2,128,288]{3,1,0,2:T(2,128)(2,1)S(1)} async-done(((bf16[2,2,128,288]{3,1,0,2:T(2,128)(2,1)}), bf16[2,2,128,288]{3,1,0,2:T(2,128)(2,1)S(1)}, u32[]{:S(2)}, u32[]{:S(2)}) %all-to-all-start) | async-done | bytes 294944 | tf_op jit(solution)/shard_map/all_to_all | solution.py:87
  89.8 17.5 %multiply_reduce_fusion = (f32[2,1152,128]{1,2,0:T(8,128)}, f32[2,1152,128]{1,2,0:T(8,128)}) fusion(f32[2,1152,32,128]{1,3,0,2:T(8,128)} %bitcast.104, f32[2,1152,32]{1,0,2:T(2,128)S(1)} %copy.112, f32[2,1152,32]{1,0,2:T(2,128)S(1)} %copy.111), kind=kLoop, calls=%fused_computation.2 | loop fusion | flops 37158912 | bytes 40697856
  116.1 13.3 %all-gather.1 = f32[4,288,2]{1,2,0:T(2,128)S(1)} all-gather(f32[1,288,2]{1,2,0:T(2,128)S(1)} %divide_bitcast_fusion), channel_id=1, replica_groups=mesh['row'=8,'col'=4] {'col'}, dimensions={0}, use_global_device_ids=true | all-gather | bytes 11520 | tf_op jit(solution)/shard_map/all_gather | solution.py:102
  131.3 13.8 %all-gather = f32[4,288,2]{1,2,0:T(2,128)S(1)} all-gather(f32[1,288,2]{1,2,0:T(2,128)S(1)} %fusion.18), channel_id=1, replica_groups=mesh['row'=8,'col'=4] {'col'}, dimensions={0}, use_global_device_ids=true | all-gather | bytes 11520 | tf_op jit(solution)/shard_map/all_gather | solution.py:101
  147.7 12.0 %psum.51 = f32[2,1152]{1,0:T(2,128)S(1)} all-reduce(f32[2,1152]{1,0:T(2,128)S(1)} %reduce_sum.77), channel_id=1, replica_groups=mesh['row'=8,'col'=4] {'col'}, use_global_device_ids=true, to_apply=%region_5.6 | all-reduce | flops 2304 | bytes 18432 | tf_op jit(solution)/shard_map/psum | solution.py:107
  166.3 55.5 %all-reduce.4.cloned.1.call-done = (f32[2,128,1152]{1,0,2:T(2,128)}, f32[2,128,1152]{1,0,2:T(2,128)}) async-done(((f32[2,128,1152]{1,0,2:T(2,128)}, f32[2,128,1152]{1,0,2:T(2,128)}), (f32[2,128,1152]{1,0,2:T(2,128)}, f32[2,128,1152]{1,0,2:T(2,128)})) %all-reduce.4.cloned.1.call-update) | async-done | bytes 2359312 | tf_op jit(solution)/shard_map/psum | solution.py:107
  221.8 7.9 %multiply_reduce_fusion.3 = (f32[2,1152]{0,1:T(8,128)S(1)}, f32[2,128,1152]{1,0,2:T(2,128)S(1)}) fusion(f32[2,1152]{0,1:T(8,128)} %copy.89, f32[2,128,1152]{1,0,2:T(2,128)} %get-tuple-element.13, f32[2,1152]{0,1:T(8,128)S(1)} %copy.77, f32[2,128,1152]{1,0,2:T(2,128)} %reshape.76, f32[2,128,1152]{1,0,2:T(2,128)} %get-tuple-element.12, f32[2,1152]{0,1:T(8,128)} %copy.86), kind=kLoop, calls=%fused_computation.16 | loop fusion | flops 2356992 | bytes 4755456 | tf_op jit(solution)/shard_map/reduce_sum | solution.py:118
  229.9 4.6 %fusion.6 = bf16[2,128,1152]{1,0,2:T(2,128)(2,1)S(1)} fusion(f32[2,128,1152]{1,0,2:T(2,128)S(1)} %copy-done.6, f32[128]{0:T(128)S(1)} %copy-done.15, f32[2,1152]{0,1:T(8,128)S(1)} %add_rsqrt_fusion, f32[2,128,1152]{1,0,2:T(2,128)S(1)} %get-tuple-element.17, f32[2,1152]{0,1:T(8,128)S(1)} %copy-done.4, f32[2,128,1152]{1,0,2:T(2,128)S(1)} %copy-done.5, ...), kind=kLoop, calls=%fused_computation.19 | loop fusion | flops 3244032 | bytes 4156928 | tf_op jit(solution)/shard_map/convert_element_type | solution.py:129
  237.2 40.9 %reduce-scatter.2.cloned.1.call-done = f32[256,288]{0,1:T(8,128)} async-done(((f32[2048,288]{0,1:T(8,128)}), f32[256,288]{0,1:T(8,128)}) %reduce-scatter.2.cloned.1.call-update) | async-done | bytes 294928 | tf_op jit(solution)/shard_map/reduce_scatter | solution.py:131
  279.1 12.5 %psum.52 = f32[288]{0:T(512)S(1)} all-reduce(f32[288]{0:T(512)S(1)} %multiply_reduce_fusion.6), channel_id=1, replica_groups=mesh['row'=8,'col'=4] {'row'}, use_global_device_ids=true, to_apply=%region_9.10 | all-reduce | flops 288 | bytes 2304 | tf_op jit(solution)/shard_map/psum | solution.py:138
  292.7 16.5 %all_gather.22 = bf16[1152,256]{1,0:T(8,128)(2,1)} all-gather(bf16[288,256]{1,0:T(8,128)(2,1)S(1)} %multiply_convert_fusion), channel_id=1, replica_groups=mesh['row'=8,'col'=4] {'col'}, dimensions={0}, use_global_device_ids=true | all-gather | bytes 737280 | tf_op jit(solution)/shard_map/all_gather | solution.py:142
  313.0 29.0 %fusion = f32[32,256,1152]{2,1,0:T(8,128)} fusion(f32[32,256,1152]{2,1,0:T(8,128)} %param.18, f32[256,1152]{1,0:T(8,128)} %bitcast.107, f32[32,2,1152]{2,1,0:T(2,128)S(1)} %copy.84, f32[256,1152]{1,0:T(8,128)S(1)} %bitcast.108), kind=kLoop, calls=%fused_computation.1 | loop fusion | flops 28311552 | bytes 78151680 | tf_op jit(solution)/shard_map/add | solution.py:116
  342.1 7.9 %all-gather.10.cloned.1.call-done = bf16[1152,2048]{1,0:T(8,128)(2,1)} async-done(((bf16[1152,256]{1,0:T(8,128)(2,1)}), bf16[1152,2048]{1,0:T(8,128)(2,1)}) %all-gather.10.cloned.1.call-update) | async-done | bytes 4718608 | tf_op jit(solution)/shard_map/all_gather | solution.py:144
  350.0 7.6 %fusion.26 = (f32[1152]{0:T(1024)S(1)}, f32[1152,640]{0,1:T(8,128)}) fusion(bf16[1152,2048]{1,0:T(8,128)(2,1)} %all-gather.10.cloned.1.call-done, bf16[2048,640]{1,0:T(8,128)(2,1)S(1)} %copy-done), kind=kOutput, calls=%fused_computation.84 | convolution fusion | flops 3020635136 | bytes 10293760 | tf_op jit(solution)/shard_map/dot_general | solution.py:143
  357.6 39.3 %pmax.7 = f32[1152]{0:T(1024)S(1)} all-reduce(f32[1152]{0:T(1024)S(1)} %get-tuple-element.25), channel_id=1, replica_groups=mesh['row'=8,'col'=4] {'row','col'}, use_global_device_ids=true, to_apply=%region_13.14 | all-reduce | flops 1152 | bytes 9216 | tf_op jit(solution)/shard_map/pmax | solution.py:155
  399.6 41.3 %all-reduce = (f32[1152]{0:T(1024)S(1)}, f32[1152]{0:T(1024)S(1)}, f32[1152]{0:T(1024)S(1)}) all-reduce(f32[1152]{0:T(1024)S(1)} %get-tuple-element.8, f32[1152]{0:T(1024)S(1)} %get-tuple-element.24, f32[1152]{0:T(1024)S(1)} %get-tuple-element.23), channel_id=1, replica_groups=mesh['row'=8,'col'=4] {'row','col'}, use_global_device_ids=true, to_apply=%region_11.12 | all-reduce | flops 3456 | bytes 27648 | tf_op jit(solution)/shard_map/psum | solution.py:157
  (135 shorter events, 52.4 us)
Async XLA Ops:
  7.2 342.8 %copy-start = (bf16[2048,640]{1,0:T(8,128)(2,1)S(1)}, bf16[2048,640]{1,0:T(8,128)(2,1)}, u32[]{:S(2)}) copy-start(bf16[2048,640]{1,0:T(8,128)(2,1)} %param.31) | copy-start | bytes 7864324
  7.2 44.6 %copy-start.8 = (bf16[288,256]{1,0:T(8,128)(2,1)S(1)}, bf16[288,256]{1,0:T(8,128)(2,1)}, u32[]{:S(2)}) copy-start(bf16[288,256]{1,0:T(8,128)(2,1)} %param.17) | copy-start | bytes 442372
  7.2 153.6 %all-gather.6.cloned.1.call-start = ((), (), s32[]{:S(2)}) async-start(), calls=%async_computation.2 | async-start | bytes 1474560 | tf_op jit(solution)/shard_map/all_gather | solution.py:99
  7.2 6.5 %collective-permute-start = (bf16[288,256]{1,0:T(8,128)(2,1)}, bf16[288,256]{1,0:T(8,128)(2,1)S(1)}, u32[]{:S(2)}, u32[]{:S(2)}) collective-permute-start(bf16[288,256]{1,0:T(8,128)(2,1)} %param.17), channel_id=1, source_target_pairs={{0,4},{4,8},{8,12},{12,16},{16,20},{20,24},{24,28},{28,0},{1,5},{5... | collective-permute-start | bytes 442376 | tf_op jit(solution)/shard_map/ppermute | solution.py:63
  13.7 5.5 %collective-permute-start.1 = (bf16[288,256]{1,0:T(8,128)(2,1)S(1)}, bf16[288,256]{1,0:T(8,128)(2,1)S(1)}, u32[]{:S(2)}, u32[]{:S(2)}) collective-permute-start(bf16[288,256]{1,0:T(8,128)(2,1)S(1)} %collective-permute-done), channel_id=1, source_target_pairs={{0,4},{4,8},{8,12},{12,16},{16,20},{20,24},{24,28},{28,0},{1,5},{5... | collective-permute-start | bytes 442376 | tf_op jit(solution)/shard_map/ppermute | solution.py:63
  19.2 5.5 %collective-permute-start.2 = (bf16[288,256]{1,0:T(8,128)(2,1)S(1)}, bf16[288,256]{1,0:T(8,128)(2,1)S(1)}, u32[]{:S(2)}, u32[]{:S(2)}) collective-permute-start(bf16[288,256]{1,0:T(8,128)(2,1)S(1)} %collective-permute-done.1), channel_id=1, source_target_pairs={{0,4},{4,8},{8,12},{12,16},{16,20},{20,24},{24,28},{28,0},{1,5},{5... | collective-permute-start | bytes 442376 | tf_op jit(solution)/shard_map/ppermute | solution.py:63
  24.6 5.5 %collective-permute-start.3 = (bf16[288,256]{1,0:T(8,128)(2,1)S(1)}, bf16[288,256]{1,0:T(8,128)(2,1)S(1)}, u32[]{:S(2)}, u32[]{:S(2)}) collective-permute-start(bf16[288,256]{1,0:T(8,128)(2,1)S(1)} %collective-permute-done.2), channel_id=1, source_target_pairs={{0,4},{4,8},{8,12},{12,16},{16,20},{20,24},{24,28},{28,0},{1,5},{5... | collective-permute-start | bytes 442376 | tf_op jit(solution)/shard_map/ppermute | solution.py:63
  30.1 5.5 %collective-permute-start.4 = (bf16[288,256]{1,0:T(8,128)(2,1)S(1)}, bf16[288,256]{1,0:T(8,128)(2,1)S(1)}, u32[]{:S(2)}, u32[]{:S(2)}) collective-permute-start(bf16[288,256]{1,0:T(8,128)(2,1)S(1)} %collective-permute-done.3), channel_id=1, source_target_pairs={{0,4},{4,8},{8,12},{12,16},{16,20},{20,24},{24,28},{28,0},{1,5},{5... | collective-permute-start | bytes 442376 | tf_op jit(solution)/shard_map/ppermute | solution.py:63
  35.6 5.6 %collective-permute-start.5 = (bf16[288,256]{1,0:T(8,128)(2,1)S(1)}, bf16[288,256]{1,0:T(8,128)(2,1)}, u32[]{:S(2)}, u32[]{:S(2)}) collective-permute-start(bf16[288,256]{1,0:T(8,128)(2,1)S(1)} %collective-permute-done.4), channel_id=1, source_target_pairs={{0,4},{4,8},{8,12},{12,16},{16,20},{20,24},{24,28},{28,0},{1,5},{5... | collective-permute-start | bytes 442376 | tf_op jit(solution)/shard_map/ppermute | solution.py:63
  41.1 5.8 %collective-permute-start.6 = (bf16[288,256]{1,0:T(8,128)(2,1)}, bf16[288,256]{1,0:T(8,128)(2,1)}, u32[]{:S(2)}, u32[]{:S(2)}) collective-permute-start(bf16[288,256]{1,0:T(8,128)(2,1)} %collective-permute-done.5), channel_id=1, source_target_pairs={{0,4},{4,8},{8,12},{12,16},{16,20},{20,24},{24,28},{28,0},{1,5},{5... | collective-permute-start | bytes 442376 | tf_op jit(solution)/shard_map/ppermute | solution.py:63
  61.7 26.2 %all-to-all-start = ((bf16[2,2,128,288]{3,1,0,2:T(2,128)(2,1)}), bf16[2,2,128,288]{3,1,0,2:T(2,128)(2,1)S(1)}, u32[]{:S(2)}, u32[]{:S(2)}) async-start(bf16[2,2,128,288]{3,1,0,2:T(2,128)(2,1)} %copy.81), calls=%async_computation | async-start | bytes 786432 | tf_op jit(solution)/shard_map/all_to_all | solution.py:87
  67.3 96.2 %all-gather.8.cloned.1.call-start = ((), (), s32[]{:S(2)}) async-start(), calls=%async_computation.3 | async-start | bytes 1474560 | tf_op jit(solution)/shard_map/all_gather | solution.py:100
  70.1 151.7 %all-reduce.4.cloned.1.call-start = ((), (), s32[]{:S(2)}) async-start(), calls=%async_computation.6 | async-start | bytes 4718592 | tf_op jit(solution)/shard_map/psum | solution.py:107
  114.1 15.4 %copy-start.12 = (bf16[2048,16]{0,1:T(8,128)(2,1)S(1)}, bf16[2048,16]{0,1:T(8,128)(2,1)}, u32[]{:S(2)}) copy-start(bf16[2048,16]{0,1:T(8,128)(2,1)} %param.24) | copy-start | bytes 196612
  114.1 163.9 %reduce-scatter.2.cloned.1.call-start = ((), (), s32[]{:S(2)}) async-start(), calls=%async_computation.4 | async-start | bytes 2654208 | tf_op jit(solution)/shard_map/reduce_scatter | solution.py:131
  221.8 8.0 %copy-start.4 = (f32[2,1152]{0,1:T(8,128)S(1)}, f32[2,1152]{0,1:T(8,128)}, u32[]{:S(2)}) copy-start(f32[2,1152]{0,1:T(8,128)} %copy.89) | copy-start | bytes 27652
  221.8 8.0 %copy-start.5 = (f32[2,128,1152]{1,0,2:T(2,128)S(1)}, f32[2,128,1152]{1,0,2:T(2,128)}, u32[]{:S(2)}) copy-start(f32[2,128,1152]{1,0,2:T(2,128)} %get-tuple-element.13) | copy-start | bytes 3538948
  221.8 8.0 %copy-start.6 = (f32[2,128,1152]{1,0,2:T(2,128)S(1)}, f32[2,128,1152]{1,0,2:T(2,128)}, u32[]{:S(2)}) copy-start(f32[2,128,1152]{1,0,2:T(2,128)} %reshape.78) | copy-start | bytes 3538948
  221.8 8.0 %copy-start.15 = (f32[128]{0:T(128)S(1)}, f32[128]{0:T(128)}, u32[]{:S(2)}) copy-start(f32[128]{0:T(128)} %param.28) | copy-start | bytes 1540
  229.7 4.8 %copy-start.3 = (f32[2,128,1152]{1,0,2:T(2,128)}, f32[2,128,1152]{1,0,2:T(2,128)S(1)}, u32[]{:S(2)}) copy-start(f32[2,128,1152]{1,0,2:T(2,128)S(1)} %get-tuple-element.17) | copy-start | bytes 3538948
  236.5 41.5 %copy-start.9 = (bf16[288,256]{1,0:T(8,128)(2,1)S(1)}, bf16[288,256]{1,0:T(8,128)(2,1)}, u32[]{:S(2)}) copy-start(bf16[288,256]{1,0:T(8,128)(2,1)} %param.17) | copy-start | bytes 442372
  236.5 113.5 %all-gather.10.cloned.1.call-start = ((), (), s32[]{:S(2)}) async-start(), calls=%async_computation.5 | async-start | bytes 5308416 | tf_op jit(solution)/shard_map/all_gather | solution.py:144
  342.1 54.8 %copy-start.13 = (s32[1152]{0:T(1024)S(1)}, s32[1152]{0:T(1024)}, u32[]{:S(2)}) copy-start(s32[1152]{0:T(1024)} %param.32) | copy-start | bytes 13828
  357.6 83.3 %copy-start.14 = (f32[1152]{0:T(1024)S(1)}, f32[1152]{0:T(1024)}, u32[]{:S(2)}) copy-start(f32[1152]{0:T(1024)} %param.33) | copy-start | bytes 13828
  (10 other events, 24.1 us)
Sparse Core Ops, SparseCore 0:
  54.9 39.4 all-gather.5
  95.9 28.5 all-gather.7
  127.0 94.8 all-reduce.3
  236.6 41.3 reduce-scatter.1
  309.4 40.5 all-gather.9
